TPU v7x, 128 devices: a whole 4x4x4 slice. The times are simulated.
128 devices in a mesh: seq: 16 (over z_lo, x, core), res: 8 (over y, z_hi).
Axes of the slice: x: 4, y: 4, z: 4 (z_hi: 2, z_lo: 2; z = z_hi * 2 + z_lo), core: 2. Of those that a mesh axis runs over, the one named last changes fastest.
Arguments:
- states: bfloat16 [512, 256, 768], P('seq', 'res'), may hold values from -6 to 6
- row_query: bfloat16 [768, 768], replicated, as said below
- row_key: bfloat16 [768, 768], replicated
- row_value: bfloat16 [768, 768], replicated, may hold values from -0.21875 to 0.21875
- row_out: bfloat16 [768, 768], replicated, may hold values from -0.21875 to 0.21875
- col_query: bfloat16 [768, 768], replicated, as said below
- col_key: bfloat16 [768, 768], replicated
- col_value: bfloat16 [768, 768], replicated, may hold values from -0.21875 to 0.21875
- col_out: bfloat16 [768, 768], replicated, may hold values from -0.21875 to 0.21875
Outputs:
- updated: bfloat16 [512, 256, 768], P('seq', 'res')
Inputs may be any that keep to these rules, and one draw needn't show every extreme that they name: No bound on the size of row_query and row_key entries or of the scores they give is promised. No bound on the size of col_query and col_key entries or of the scores they give is promised.
All inputs are finite; a program needn't handle non-finite values.
Results may differ from a plain program's by a relative error of at most 0.02.
Values may be sent and summed in bfloat16 or wider, within the bound.
A program may use at most 128 MiB of HBM per device.

v0:
```python
import math
import jax
import jax.numpy as jnp
from jax import lax
from jax.sharding import PartitionSpec as P

D = 768
HEADS = 12


def normalize(states):
    values = states.astype(jnp.float32)
    center = values - jnp.mean(values, axis=-1, keepdims=True)
    spread = jnp.mean(center * center, axis=-1, keepdims=True)
    return (center * lax.rsqrt(spread + 1e-05)).astype(jnp.bfloat16)


def project(inputs, weight):
    return jnp.dot(inputs, weight, preferred_element_type=jnp.float32)


def split_heads(field):
    return field.reshape(field.shape[0], field.shape[1], HEADS, D // HEADS)


def on_device(
    states, row_query, row_key, row_value, row_out, col_query, col_key, col_value, col_out
):
    row_count, col_count = (states.shape[0], states.shape[1])
    head_dim = D // HEADS
    all_rows = row_count * lax.axis_size("seq")
    tied_scale = head_dim ** (-0.5) / math.sqrt(all_rows)
    normed = normalize(states)
    q1 = project(normed, row_query).astype(jnp.bfloat16)
    k1 = project(normed, row_key).astype(jnp.bfloat16)
    v1 = project(normed, row_value).astype(jnp.bfloat16)
    q_moved, k_moved, v_moved = (
        lax.all_to_all(q1, "res", split_axis=0, concat_axis=1, tiled=True),
        lax.all_to_all(k1, "res", split_axis=0, concat_axis=1, tiled=True),
        lax.all_to_all(v1, "res", split_axis=0, concat_axis=1, tiled=True),
    )
    partial_value = (
        jnp.einsum(
            "rihd,rjhd->hij",
            split_heads(q_moved),
            split_heads(k_moved),
            preferred_element_type=jnp.float32,
        )
        * tied_scale
    )
    tied = lax.psum(partial_value, ("seq", "res"))
    prob1 = jax.nn.softmax(tied, axis=-1).astype(jnp.bfloat16)
    o_moved = jnp.einsum(
        "hij,rjhd->rihd", prob1, split_heads(v_moved), preferred_element_type=jnp.float32
    ).astype(jnp.bfloat16)
    o_moved = o_moved.reshape(o_moved.shape[0], o_moved.shape[1], D)
    o1 = lax.all_to_all(o_moved, "res", split_axis=1, concat_axis=0, tiled=True)
    mid = (states.astype(jnp.float32) + project(o1, row_out)).astype(jnp.bfloat16)
    normed2 = normalize(mid)
    q2 = project(normed2, col_query).astype(jnp.bfloat16)
    k2 = project(normed2, col_key).astype(jnp.bfloat16)
    v2 = project(normed2, col_value).astype(jnp.bfloat16)
    q_cols, k_cols, v_cols = (
        lax.all_to_all(q2, "seq", split_axis=1, concat_axis=0, tiled=True),
        lax.all_to_all(k2, "seq", split_axis=1, concat_axis=0, tiled=True),
        lax.all_to_all(v2, "seq", split_axis=1, concat_axis=0, tiled=True),
    )
    gathered_rows, local_cols = (q_cols.shape[0], q_cols.shape[1])

    def arrange(field):
        return field.reshape(gathered_rows, local_cols, HEADS, head_dim).transpose(1, 0, 2, 3)

    def attend(triple):
        query_col, key_col, value_col = triple
        score = jnp.einsum(
            "rhd,shd->hrs", query_col, key_col, preferred_element_type=jnp.float32
        ) * head_dim ** (-0.5)
        prob2 = jax.nn.softmax(score, axis=-1).astype(jnp.bfloat16)
        return jnp.einsum(
            "hrs,shd->rhd", prob2, value_col, preferred_element_type=jnp.float32
        ).astype(jnp.bfloat16)

    o2 = lax.map(attend, (arrange(q_cols), arrange(k_cols), arrange(v_cols)))
    o2 = o2.reshape(local_cols, gathered_rows, D).transpose(1, 0, 2)
    colupd = project(o2, col_out).astype(jnp.bfloat16)
    colupd = lax.all_to_all(colupd, "seq", split_axis=0, concat_axis=1, tiled=True)
    return (mid.astype(jnp.float32) + colupd.astype(jnp.float32)).astype(jnp.bfloat16)


def solution(mesh):
    placed = (P("seq", "res", None), P(), P(), P(), P(), P(), P(), P(), P())
    return jax.shard_map(
        on_device, mesh=mesh, in_specs=placed, out_specs=P("seq", "res", None), check_vma=False
    )
```

profile of v0, /device:TPU:1, one launch (start us, length us, event | category | flops | bytes accessed | tf_op | source)
XLA Modules:
  0.0 487.7 jit_solution(7350773890253013936)
XLA Ops:
  11.7 8.3 %all-to-all-start.1 = ((bf16[32,32,768]{2,1,0:T(8,128)(2,1)}), bf16[32,32,768]{2,1,0:T(8,128)(2,1)}, u32[]{:S(2)}, u32[]{:S(2)}) async-start(bf16[32,32,768]{2,1,0:T(8,128)(2,1)} %convolution_convert_fusion.5), calls=%async_computation.1 | async-start | bytes 3145728 | tf_op jit(solution)/shard_map/all_to_all | solution.py:38
  23.9 19.3 %all-to-all-done.1 = bf16[32,32,768]{2,1,0:T(8,128)(2,1)} async-done(((bf16[32,32,768]{2,1,0:T(8,128)(2,1)}), bf16[32,32,768]{2,1,0:T(8,128)(2,1)}, u32[]{:S(2)}, u32[]{:S(2)}) %all-to-all-start.1) | async-done | bytes 1572896 | tf_op jit(solution)/shard_map/all_to_all | solution.py:38
  50.3 5.9 %reshape.63 = bf16[4,256,12,64]{3,2,1,0:T(8,128)(2,1)} reshape(bf16[4,8,32,768]{3,2,1,0:T(8,128)(2,1)} %bitcast.147) | data formatting | bytes 3145728 | tf_op jit(solution)/shard_map/reshape | solution.py:23
  56.2 13.5 %all-to-all-done.2 = bf16[32,32,768]{2,1,0:T(8,128)(2,1)} async-done(((bf16[32,32,768]{2,1,0:T(8,128)(2,1)}), bf16[32,32,768]{2,1,0:T(8,128)(2,1)}, u32[]{:S(2)}, u32[]{:S(2)}) %all-to-all-start.2) | async-done | bytes 1572896 | tf_op jit(solution)/shard_map/all_to_all | solution.py:39
  72.3 5.9 %reshape.64 = bf16[4,256,12,64]{3,2,1,0:T(8,128)(2,1)} reshape(bf16[4,8,32,768]{3,2,1,0:T(8,128)(2,1)} %bitcast.148) | data formatting | bytes 3145728 | tf_op jit(solution)/shard_map/reshape | solution.py:23
  78.2 6.7 %bitcast_multiply_fusion = f32[12,256,256]{2,1,0:T(8,128)} fusion(bf16[4,256,12,64]{3,2,1,0:T(8,128)(2,1)} %reshape.64, bf16[4,256,12,64]{3,2,1,0:T(8,128)(2,1)} %reshape.63), kind=kOutput, calls=%fused_computation.43 | convolution fusion | flops 403439616 | bytes 6291456 | tf_op jit(solution)/shard_map/rihd,rjhd->hij/dot_general | solution.py:43
  87.7 26.8 %all_to_all.117 = bf16[32,32,768]{2,1,0:T(8,128)(2,1)S(1)} all-to-all(bf16[32,32,768]{2,1,0:T(8,128)(2,1)S(1)} %convolution_convert_fusion.6), channel_id=1, replica_groups=mesh['seq'=16,'res'=8] {'res'}, dimensions={0} | all-to-all | bytes 3145728 | tf_op jit(solution)/shard_map/all_to_all | solution.py:40
  115.8 5.9 %reshape.62 = bf16[4,256,12,64]{3,2,1,0:T(8,128)(2,1)} reshape(bf16[4,8,32,768]{3,2,1,0:T(8,128)(2,1)} %bitcast.149) | data formatting | bytes 3145728 | tf_op jit(solution)/shard_map/reshape | solution.py:23
  121.7 123.8 %all-reduce.2.cloned.1.call-done = f32[12,256,256]{2,1,0:T(8,128)} async-done(((f32[12,256,256]{2,1,0:T(8,128)}), f32[12,256,256]{2,1,0:T(8,128)}) %all-reduce.2.cloned.1.call-update) | async-done | bytes 3145744 | tf_op jit(solution)/shard_map/psum | solution.py:51
  249.3 12.5 %fusion.63 = bf16[4,256,12,64]{1,3,0,2:T(8,128)(2,1)} fusion(f32[12,256]{1,0:T(8,128)S(1)} %fusion.92, bf16[4,256,12,64]{3,2,1,0:T(8,128)(2,1)} %reshape.62, f32[12,256,256]{2,1,0:T(8,128)} %all-reduce.2.cloned.1.call-done), kind=kOutput, calls=%fused_computation.68 | convolution fusion | flops 405802240 | bytes 6303744 | tf_op jit(solution)/shard_map/hij,rjhd->rihd/dot_general | solution.py:53
  268.2 25.9 %all_to_all.118 = bf16[4,256,768]{2,0,1:T(4,128)(2,1)S(1)} all-to-all(bf16[4,256,768]{2,0,1:T(4,128)(2,1)} %copy.42), channel_id=1, replica_groups=mesh['seq'=16,'res'=8] {'res'}, dimensions={1} | all-to-all | bytes 3145728 | tf_op jit(solution)/shard_map/all_to_all | solution.py:57
  301.3 6.3 %all-to-all-start.6 = ((bf16[32,32,768]{2,0,1:T(8,128)(2,1)}), bf16[32,32,768]{2,0,1:T(8,128)(2,1)S(1)}, u32[]{:S(2)}, u32[]{:S(2)}) async-start(bf16[32,32,768]{2,0,1:T(8,128)(2,1)} %copy.49), calls=%async_computation.6 | async-start | bytes 3145728 | tf_op jit(solution)/shard_map/all_to_all | solution.py:65
  312.9 16.3 %all-to-all-done.6 = bf16[32,32,768]{2,0,1:T(8,128)(2,1)S(1)} async-done(((bf16[32,32,768]{2,0,1:T(8,128)(2,1)}), bf16[32,32,768]{2,0,1:T(8,128)(2,1)S(1)}, u32[]{:S(2)}, u32[]{:S(2)}) %all-to-all-start.6) | async-done | bytes 1572896 | tf_op jit(solution)/shard_map/all_to_all | solution.py:65
  339.3 16.4 %all-to-all-done.5 = bf16[32,32,768]{2,0,1:T(8,128)(2,1)} async-done(((bf16[32,32,768]{2,0,1:T(8,128)(2,1)}), bf16[32,32,768]{2,0,1:T(8,128)(2,1)}, u32[]{:S(2)}, u32[]{:S(2)}) %all-to-all-start.5) | async-done | bytes 1572896 | tf_op jit(solution)/shard_map/all_to_all | solution.py:64
  355.7 13.4 %all-to-all-start.4 = ((bf16[32,32,768]{2,0,1:T(8,128)(2,1)}), bf16[32,32,768]{2,0,1:T(8,128)(2,1)}, u32[]{:S(2)}, u32[]{:S(2)}) async-start(bf16[32,32,768]{2,0,1:T(8,128)(2,1)} %copy.45), calls=%async_computation.4 | async-start | bytes 3145728 | tf_op jit(solution)/shard_map/all_to_all | solution.py:66
  370.4 5.9 %reshape.68 = bf16[512,2,12,64]{3,2,0,1:T(8,128)(2,1)} reshape(bf16[16,32,2,768]{3,1,0,2:T(8,128)(2,1)} %bitcast.150) | data formatting | bytes 3145728 | tf_op jit(solution)/shard_map/reshape | solution.py:71
  397.8 5.5 %copy.51 = bf16[2,512,12,64]{1,3,2,0:T(8,128)(2,1)} copy(bf16[2,512,12,64]{3,2,1,0:T(8,128)(2,1)} %bitcast.142) | data formatting | bytes 3145728 | tf_op jit(solution)/shard_map/while | solution.py:83
  403.2 32.3 %while.10 = (s32[]{:T(128)}, bf16[2,512,12,64]{1,3,2,0:T(8,128)(2,1)S(1)}, bf16[2,512,12,64]{1,3,2,0:T(8,128)(2,1)}, bf16[2,512,12,64]{1,3,2,0:T(8,128)(2,1)}, bf16[2,512,12,64]{1,3,2,0:T(8,128)(2,1)}, /*index=5*/s32[]{:T(128)}) while((s32[]{:T(128)}, bf16[2,512,12,64]{1,3,2,0:T(8,128)(2,1)S(1)}, bf16[2,512,12,64]{1,3,2,0:T(8,128)(2,1)}, ...), condition=%wide.region_10.11_spmd, body=%wide.region_7.10_spmd.sunk | while | flops 821428736 | bytes 28371012 | solution.py:83
  403.2 10.1 %fusion.105 = (f32[12,512]{1,0:T(8,128)S(1)}, f32[12,512,512]{1,2,0:T(8,128)}) fusion(bf16[2,512,12,64]{1,3,2,0:T(8,128)(2,1)} %get-tuple-element.108, s32[]{:T(128)} %get-tuple-element.98, bf16[2,512,12,64]{1,3,2,0:T(8,128)(2,1)} %get-tuple-element.107), kind=kOutput, calls=%fused_computation.82.clone.1 | convolution fusion | flops 412090880 | bytes 14181376 | tf_op jit(solution)/shard_map/while/body/eval_jaxpr/sub | solution.py:78
  413.3 6.0 %fusion.106 = bf16[2,512,12,64]{1,3,2,0:T(8,128)(2,1)S(1)} fusion(bf16[2,512,12,64]{1,3,2,0:T(8,128)(2,1)S(1)} %get-tuple-element.99, s32[]{:T(128)} %get-tuple-element.98, f32[12,512,512]{1,2,0:T(8,128)} %get-tuple-element.90, f32[12,512]{1,0:T(8,128)S(1)} %get-tuple-element.91, bf16[2,512,12,64]{1,3,2,0:T(8,128)(2,1)} %get-tuple-element.106), kind=kOutput, calls=%fused_computation.10.clone.1 | convolution fusion | flops 409337856 | bytes 14189568 | tf_op jit(solution)/shard_map/while/body/eval_jaxpr/hrs,shd->rhd/dot_general | solution.py:79
  419.4 10.1 %fusion.105 = (f32[12,512]{1,0:T(8,128)S(1)}, f32[12,512,512]{1,2,0:T(8,128)}) fusion(bf16[2,512,12,64]{1,3,2,0:T(8,128)(2,1)} %get-tuple-element.108, s32[]{:T(128)} %get-tuple-element.98, bf16[2,512,12,64]{1,3,2,0:T(8,128)(2,1)} %get-tuple-element.107), kind=kOutput, calls=%fused_computation.82.clone.1 | convolution fusion | flops 412090880 | bytes 14181376 | tf_op jit(solution)/shard_map/while/body/eval_jaxpr/sub | solution.py:78
  429.4 6.0 %fusion.106 = bf16[2,512,12,64]{1,3,2,0:T(8,128)(2,1)S(1)} fusion(bf16[2,512,12,64]{1,3,2,0:T(8,128)(2,1)S(1)} %get-tuple-element.99, s32[]{:T(128)} %get-tuple-element.98, f32[12,512,512]{1,2,0:T(8,128)} %get-tuple-element.90, f32[12,512]{1,0:T(8,128)S(1)} %get-tuple-element.91, bf16[2,512,12,64]{1,3,2,0:T(8,128)(2,1)} %get-tuple-element.106), kind=kOutput, calls=%fused_computation.10.clone.1 | convolution fusion | flops 409337856 | bytes 14189568 | tf_op jit(solution)/shard_map/while/body/eval_jaxpr/hrs,shd->rhd/dot_general | solution.py:79
  441.5 26.7 %all_to_all.119 = bf16[512,2,768]{2,1,0:T(2,128)(2,1)S(1)} all-to-all(bf16[512,2,768]{2,1,0:T(2,128)(2,1)S(1)} %copy.55), channel_id=1, replica_groups=mesh['seq'=16,'res'=8] {'seq'}, dimensions={0} | all-to-all | bytes 3145728 | tf_op jit(solution)/shard_map/all_to_all | solution.py:86
  471.6 5.4 %reshape.70 = f32[32,32,768]{2,1,0:T(8,128)} reshape(f32[32,16,2,768]{3,2,1,0:T(2,128)} %copy_bitcast_fusion) | data formatting | bytes 6291456 | tf_op jit(solution)/shard_map/convert_element_type | solution.py:87
  (61 shorter events, 91.2 us)
Async XLA Ops:
  6.5 287.9 %copy-start = (bf16[768,768]{1,0:T(8,128)(2,1)S(1)}, bf16[768,768]{1,0:T(8,128)(2,1)}, u32[]{:S(2)}) copy-start(bf16[768,768]{1,0:T(8,128)(2,1)} %param.15) | copy-start | bytes 3538948
  6.5 2.0 copy-start.2
  6.5 2.6 copy-start.6
  11.7 31.5 %all-to-all-start.1 = ((bf16[32,32,768]{2,1,0:T(8,128)(2,1)}), bf16[32,32,768]{2,1,0:T(8,128)(2,1)}, u32[]{:S(2)}, u32[]{:S(2)}) async-start(bf16[32,32,768]{2,1,0:T(8,128)(2,1)} %convolution_convert_fusion.5), calls=%async_computation.1 | async-start | bytes 3145728 | tf_op jit(solution)/shard_map/all_to_all | solution.py:38
  43.2 26.4 %all-to-all-start.2 = ((bf16[32,32,768]{2,1,0:T(8,128)(2,1)}), bf16[32,32,768]{2,1,0:T(8,128)(2,1)}, u32[]{:S(2)}, u32[]{:S(2)}) async-start(bf16[32,32,768]{2,1,0:T(8,128)(2,1)} %convolution_convert_fusion.4), calls=%async_computation.2 | async-start | bytes 3145728 | tf_op jit(solution)/shard_map/all_to_all | solution.py:39
  47.5 198.0 %all-reduce.2.cloned.1.call-start = ((), (), s32[]{:S(2)}) async-start(), calls=%async_computation.8 | async-start | bytes 6291456 | tf_op jit(solution)/shard_map/psum | solution.py:51
  295.9 3.4 copy-start.3
  296.0 1.8 copy-start.7
  301.3 27.8 %all-to-all-start.6 = ((bf16[32,32,768]{2,0,1:T(8,128)(2,1)}), bf16[32,32,768]{2,0,1:T(8,128)(2,1)S(1)}, u32[]{:S(2)}, u32[]{:S(2)}) async-start(bf16[32,32,768]{2,0,1:T(8,128)(2,1)} %copy.49), calls=%async_computation.6 | async-start | bytes 3145728 | tf_op jit(solution)/shard_map/all_to_all | solution.py:65
  329.1 26.5 %all-to-all-start.5 = ((bf16[32,32,768]{2,0,1:T(8,128)(2,1)}), bf16[32,32,768]{2,0,1:T(8,128)(2,1)}, u32[]{:S(2)}, u32[]{:S(2)}) async-start(bf16[32,32,768]{2,0,1:T(8,128)(2,1)} %copy.47), calls=%async_computation.5 | async-start | bytes 3145728 | tf_op jit(solution)/shard_map/all_to_all | solution.py:64
  355.7 36.7 %all-to-all-start.4 = ((bf16[32,32,768]{2,0,1:T(8,128)(2,1)}), bf16[32,32,768]{2,0,1:T(8,128)(2,1)}, u32[]{:S(2)}, u32[]{:S(2)}) async-start(bf16[32,32,768]{2,0,1:T(8,128)(2,1)} %copy.45), calls=%async_computation.4 | async-start | bytes 3145728 | tf_op jit(solution)/shard_map/all_to_all | solution.py:66
  397.8 5.5 %copy-start.5 = (bf16[2,512,12,64]{1,3,2,0:T(8,128)(2,1)S(1)}, bf16[2,512,12,64]{1,3,2,0:T(8,128)(2,1)}, u32[]{:S(2)}) copy-start(bf16[2,512,12,64]{1,3,2,0:T(8,128)(2,1)} %custom-call) | copy-start | bytes 4718596
  435.5 1.6 copy-start.8
  471.6 5.4 %copy-start.4 = (bf16[32,32,768]{2,1,0:T(8,128)(2,1)S(1)}, bf16[32,32,768]{2,1,0:T(8,128)(2,1)}, u32[]{:S(2)}) copy-start(bf16[32,32,768]{2,1,0:T(8,128)(2,1)} %copy-done.3) | copy-start | bytes 4718596
  477.0 3.6 copy-start.1
Sparse Core Ops, SparseCore 0:
  85.1 160.3 all-reduce.1
where the time goes:
time: 496 us; the launch traced here: 488 us
  waiting for transfers between devices  189 us (38%)
  local copies, waits for them, and re-layouts  81.2 us (16%)
  blocking collectives  79.4 us (16%)
  matrix products  72.8 us (15%)
  starting transfers between devices  37.3 us (8%)
  between operations  13.9 us (3%)
  other arithmetic  13.8 us (3%)
    psum x1, waiting for transfers between devices, on_device(): tied = lax.psum(partial_value, ('seq', 'res'))  124 us
    all_to_all x1, blocking collectives, on_device(): lax.all_to_all(v1, 'res', split_axis=0, concat_axis=1, tiled=True)  26.8 us
    all_to_all x1, blocking collectives, on_device(): lax.all_to_all(colupd, 'seq', split_axis=0, concat_axis=1, tiled=True)  26.7 us
    all_to_all x1, blocking collectives, on_device(): o1 = lax.all_to_all(o_moved, 'res', split_axis=1, concat_axis=0, tiled=True)  25.9 us
    dot_general x8, matrix products, project(): return jnp.dot(inputs, weight, preferred_element_type=jnp.float32)  21.4 us
    sub x2, matrix products, attend(): prob2 = jax.nn.softmax(score, axis=-1).astype(jnp.bfloat16)  20.1 us
    all_to_all x1, waiting for transfers between devices, on_device(): lax.all_to_all(q1, 'res', split_axis=0, concat_axis=1, tiled=True)  19.3 us
    reshape x3, local copies, waits for them, and re-layouts, split_heads(): return field.reshape(field.shape[0], field.shape[1], HEADS, D // HEADS)  17.7 us
  transfers between devices with their start and end apart: 6, of which 5 were waited for; matrix products, arithmetic and copies ran while one was open for 11% of the time, Pallas kernels for 0%

commit v1 on v0

--- a/solution.py
+++ b/solution.py
@@ -48,7 +48,7 @@
         )
         * tied_scale
     )
-    tied = lax.psum(partial_value, ("seq", "res"))
+    tied = lax.psum(lax.psum(partial_value, "seq"), "res")
     prob1 = jax.nn.softmax(tied, axis=-1).astype(jnp.bfloat16)
     o_moved = jnp.einsum(
         "hij,rjhd->rihd", prob1, split_heads(v_moved), preferred_element_type=jnp.float32

time: 496 us -> 624 us (1.26)
  waiting for transfers between devices: 189 us -> 310 us
  blocking collectives: 79.4 us -> 86.2 us
    psum x1 -> x2, waiting for transfers between devices: 124 us -> 245 us  [on_device(): tied = lax.psum(lax.psum(partial_value, 'seq'), 'res')]
  transfers between devices with their start and end apart: 6 -> 7, of which waited for: 5 -> 6; matrix products, arithmetic and copies ran while one was open for 11% -> 9% of each run, Pallas kernels for 0% -> 0%
where the time goes in v1:
time: 624 us; the launch traced here: 616 us
  waiting for transfers between devices  310 us (50%)
  blocking collectives  86.2 us (14%)
  local copies, waits for them, and re-layouts  81.2 us (13%)
  matrix products  72.8 us (12%)
  starting transfers between devices  38.1 us (6%)
  between operations  13.9 us (2%)
  other arithmetic  13.8 us (2%)
    psum x2, waiting for transfers between devices, on_device(): tied = lax.psum(lax.psum(partial_value, 'seq'), 'res')  245 us
    all_to_all x1, blocking collectives, on_device(): lax.all_to_all(v1, 'res', split_axis=0, concat_axis=1, tiled=True)  30.8 us
    all_to_all x1, blocking collectives, on_device(): o1 = lax.all_to_all(o_moved, 'res', split_axis=1, concat_axis=0, tiled=True)  28.7 us
    all_to_all x1, blocking collectives, on_device(): lax.all_to_all(colupd, 'seq', split_axis=0, concat_axis=1, tiled=True)  26.7 us
    dot_general x8, matrix products, project(): return jnp.dot(inputs, weight, preferred_element_type=jnp.float32)  21.4 us
    sub x2, matrix products, attend(): prob2 = jax.nn.softmax(score, axis=-1).astype(jnp.bfloat16)  20.1 us
    all_to_all x1, waiting for transfers between devices, on_device(): lax.all_to_all(q1, 'res', split_axis=0, concat_axis=1, tiled=True)  19.3 us
    reshape x3, local copies, waits for them, and re-layouts, split_heads(): return field.reshape(field.shape[0], field.shape[1], HEADS, D // HEADS)  17.6 us
  transfers between devices with their start and end apart: 7, of which 6 were waited for; matrix products, arithmetic and copies ran while one was open for 9% of the time, Pallas kernels for 0%

profile of v1, /device:TPU:1, one launch (start us, length us, event | category | flops | bytes accessed | tf_op | source)
XLA Modules:
  0.0 616.1 jit_solution(1011375208847591836)
XLA Ops:
  11.7 8.3 %all-to-all-start.1 = ((bf16[32,32,768]{2,1,0:T(8,128)(2,1)}), bf16[32,32,768]{2,1,0:T(8,128)(2,1)}, u32[]{:S(2)}, u32[]{:S(2)}) async-start(bf16[32,32,768]{2,1,0:T(8,128)(2,1)} %convolution_convert_fusion.5), calls=%async_computation.1 | async-start | bytes 3145728 | tf_op jit(solution)/shard_map/all_to_all | solution.py:38
  23.9 19.3 %all-to-all-done.1 = bf16[32,32,768]{2,1,0:T(8,128)(2,1)} async-done(((bf16[32,32,768]{2,1,0:T(8,128)(2,1)}), bf16[32,32,768]{2,1,0:T(8,128)(2,1)}, u32[]{:S(2)}, u32[]{:S(2)}) %all-to-all-start.1) | async-done | bytes 1572896 | tf_op jit(solution)/shard_map/all_to_all | solution.py:38
  50.3 5.9 reshape.63
  56.2 13.5 %all-to-all-done.2 = bf16[32,32,768]{2,1,0:T(8,128)(2,1)} async-done(((bf16[32,32,768]{2,1,0:T(8,128)(2,1)}), bf16[32,32,768]{2,1,0:T(8,128)(2,1)}, u32[]{:S(2)}, u32[]{:S(2)}) %all-to-all-start.2) | async-done | bytes 1572896 | tf_op jit(solution)/shard_map/all_to_all | solution.py:39
  72.3 5.9 reshape.64
  78.2 6.7 %bitcast_multiply_fusion = f32[12,256,256]{2,1,0:T(8,128)} fusion(bf16[4,256,12,64]{3,2,1,0:T(8,128)(2,1)} %reshape.64, bf16[4,256,12,64]{3,2,1,0:T(8,128)(2,1)} %reshape.63), kind=kOutput, calls=%fused_computation.43 | convolution fusion | flops 403439616 | bytes 6291456 | tf_op jit(solution)/shard_map/rihd,rjhd->hij/dot_general | solution.py:43
  85.0 124.3 %all-reduce.3.cloned.1.call-done = f32[12,256,256]{2,1,0:T(8,128)} async-done(((f32[12,256,256]{2,1,0:T(8,128)}), f32[12,256,256]{2,1,0:T(8,128)}) %all-reduce.3.cloned.1.call-update) | async-done | bytes 3145744 | tf_op jit(solution)/shard_map/psum | solution.py:51
  212.1 30.8 %all_to_all.117 = bf16[32,32,768]{2,1,0:T(8,128)(2,1)S(1)} all-to-all(bf16[32,32,768]{2,1,0:T(8,128)(2,1)S(1)} %convolution_convert_fusion.6), channel_id=1, replica_groups=mesh['seq'=16,'res'=8] {'res'}, dimensions={0} | all-to-all | bytes 3145728 | tf_op jit(solution)/shard_map/all_to_all | solution.py:40
  244.1 5.9 reshape.62
  250.0 120.3 %all-reduce.5.cloned.1.call-done = f32[12,256,256]{2,1,0:T(8,128)} async-done(((f32[12,256,256]{2,1,0:T(8,128)}), f32[12,256,256]{2,1,0:T(8,128)}) %all-reduce.5.cloned.1.call-update) | async-done | bytes 3145744 | tf_op jit(solution)/shard_map/psum | solution.py:51
  374.0 12.5 %fusion.63 = bf16[4,256,12,64]{1,3,0,2:T(8,128)(2,1)} fusion(f32[12,256]{1,0:T(8,128)S(1)} %fusion.92, bf16[4,256,12,64]{3,2,1,0:T(8,128)(2,1)} %reshape.62, f32[12,256,256]{2,1,0:T(8,128)} %all-reduce.5.cloned.1.call-done), kind=kOutput, calls=%fused_computation.68 | convolution fusion | flops 405802240 | bytes 6303744 | tf_op jit(solution)/shard_map/hij,rjhd->rihd/dot_general | solution.py:53
  393.0 28.7 %all_to_all.118 = bf16[4,256,768]{2,0,1:T(4,128)(2,1)S(1)} all-to-all(bf16[4,256,768]{2,0,1:T(4,128)(2,1)} %copy.42), channel_id=1, replica_groups=mesh['seq'=16,'res'=8] {'res'}, dimensions={1} | all-to-all | bytes 3145728 | tf_op jit(solution)/shard_map/all_to_all | solution.py:57
  428.9 7.1 %all-to-all-start.6 = ((bf16[32,32,768]{2,0,1:T(8,128)(2,1)}), bf16[32,32,768]{2,0,1:T(8,128)(2,1)S(1)}, u32[]{:S(2)}, u32[]{:S(2)}) async-start(bf16[32,32,768]{2,0,1:T(8,128)(2,1)} %copy.49), calls=%async_computation.6 | async-start | bytes 3145728 | tf_op jit(solution)/shard_map/all_to_all | solution.py:65
  441.2 16.3 %all-to-all-done.6 = bf16[32,32,768]{2,0,1:T(8,128)(2,1)S(1)} async-done(((bf16[32,32,768]{2,0,1:T(8,128)(2,1)}), bf16[32,32,768]{2,0,1:T(8,128)(2,1)S(1)}, u32[]{:S(2)}, u32[]{:S(2)}) %all-to-all-start.6) | async-done | bytes 1572896 | tf_op jit(solution)/shard_map/all_to_all | solution.py:65
  467.6 16.4 %all-to-all-done.5 = bf16[32,32,768]{2,0,1:T(8,128)(2,1)} async-done(((bf16[32,32,768]{2,0,1:T(8,128)(2,1)}), bf16[32,32,768]{2,0,1:T(8,128)(2,1)}, u32[]{:S(2)}, u32[]{:S(2)}) %all-to-all-start.5) | async-done | bytes 1572896 | tf_op jit(solution)/shard_map/all_to_all | solution.py:64
  484.0 13.4 %all-to-all-start.4 = ((bf16[32,32,768]{2,0,1:T(8,128)(2,1)}), bf16[32,32,768]{2,0,1:T(8,128)(2,1)}, u32[]{:S(2)}, u32[]{:S(2)}) async-start(bf16[32,32,768]{2,0,1:T(8,128)(2,1)} %copy.45), calls=%async_computation.4 | async-start | bytes 3145728 | tf_op jit(solution)/shard_map/all_to_all | solution.py:66
  498.8 5.9 reshape.68
  526.1 5.5 copy.51
  531.5 32.3 %while.10 = (s32[]{:T(128)}, bf16[2,512,12,64]{1,3,2,0:T(8,128)(2,1)S(1)}, bf16[2,512,12,64]{1,3,2,0:T(8,128)(2,1)}, bf16[2,512,12,64]{1,3,2,0:T(8,128)(2,1)}, bf16[2,512,12,64]{1,3,2,0:T(8,128)(2,1)}, /*index=5*/s32[]{:T(128)}) while((s32[]{:T(128)}, bf16[2,512,12,64]{1,3,2,0:T(8,128)(2,1)S(1)}, bf16[2,512,12,64]{1,3,2,0:T(8,128)(2,1)}, ...), condition=%wide.region_11.12_spmd, body=%wide.region_8.11_spmd.sunk | while | flops 821428736 | bytes 28371012 | solution.py:83
  531.5 10.1 %fusion.105 = (f32[12,512]{1,0:T(8,128)S(1)}, f32[12,512,512]{1,2,0:T(8,128)}) fusion(bf16[2,512,12,64]{1,3,2,0:T(8,128)(2,1)} %get-tuple-element.108, s32[]{:T(128)} %get-tuple-element.98, bf16[2,512,12,64]{1,3,2,0:T(8,128)(2,1)} %get-tuple-element.107), kind=kOutput, calls=%fused_computation.82.clone.1 | convolution fusion | flops 412090880 | bytes 14181376 | tf_op jit(solution)/shard_map/while/body/eval_jaxpr/sub | solution.py:78
  541.6 6.0 fusion.106
  547.7 10.1 %fusion.105 = (f32[12,512]{1,0:T(8,128)S(1)}, f32[12,512,512]{1,2,0:T(8,128)}) fusion(bf16[2,512,12,64]{1,3,2,0:T(8,128)(2,1)} %get-tuple-element.108, s32[]{:T(128)} %get-tuple-element.98, bf16[2,512,12,64]{1,3,2,0:T(8,128)(2,1)} %get-tuple-element.107), kind=kOutput, calls=%fused_computation.82.clone.1 | convolution fusion | flops 412090880 | bytes 14181376 | tf_op jit(solution)/shard_map/while/body/eval_jaxpr/sub | solution.py:78
  557.8 6.0 fusion.106
  569.8 26.7 %all_to_all.119 = bf16[512,2,768]{2,1,0:T(2,128)(2,1)S(1)} all-to-all(bf16[512,2,768]{2,1,0:T(2,128)(2,1)S(1)} %copy.55), channel_id=1, replica_groups=mesh['seq'=16,'res'=8] {'seq'}, dimensions={0} | all-to-all | bytes 3145728 | tf_op jit(solution)/shard_map/all_to_all | solution.py:86
  (64 shorter events, 96.7 us)
Async XLA Ops:
  6.5 415.5 %copy-start = (bf16[768,768]{1,0:T(8,128)(2,1)S(1)}, bf16[768,768]{1,0:T(8,128)(2,1)}, u32[]{:S(2)}) copy-start(bf16[768,768]{1,0:T(8,128)(2,1)} %param.15) | copy-start | bytes 3538948
  6.5 2.0 copy-start.2
  6.5 2.6 copy-start.6
  11.7 31.5 %all-to-all-start.1 = ((bf16[32,32,768]{2,1,0:T(8,128)(2,1)}), bf16[32,32,768]{2,1,0:T(8,128)(2,1)}, u32[]{:S(2)}, u32[]{:S(2)}) async-start(bf16[32,32,768]{2,1,0:T(8,128)(2,1)} %convolution_convert_fusion.5), calls=%async_computation.1 | async-start | bytes 3145728 | tf_op jit(solution)/shard_map/all_to_all | solution.py:38
  43.2 26.4 %all-to-all-start.2 = ((bf16[32,32,768]{2,1,0:T(8,128)(2,1)}), bf16[32,32,768]{2,1,0:T(8,128)(2,1)}, u32[]{:S(2)}, u32[]{:S(2)}) async-start(bf16[32,32,768]{2,1,0:T(8,128)(2,1)} %convolution_convert_fusion.4), calls=%async_computation.2 | async-start | bytes 3145728 | tf_op jit(solution)/shard_map/all_to_all | solution.py:39
  47.5 161.8 %all-reduce.3.cloned.1.call-start = ((), (), s32[]{:S(2)}) async-start(), calls=%async_computation.8 | async-start | bytes 6291456 | tf_op jit(solution)/shard_map/psum | solution.py:51
  85.0 285.3 %all-reduce.5.cloned.1.call-start = ((), (), s32[]{:S(2)}) async-start(), calls=%async_computation.9 | async-start | bytes 6291456 | tf_op jit(solution)/shard_map/psum | solution.py:51
  423.5 3.3 copy-start.3
  423.5 1.8 copy-start.7
  428.9 28.6 %all-to-all-start.6 = ((bf16[32,32,768]{2,0,1:T(8,128)(2,1)}), bf16[32,32,768]{2,0,1:T(8,128)(2,1)S(1)}, u32[]{:S(2)}, u32[]{:S(2)}) async-start(bf16[32,32,768]{2,0,1:T(8,128)(2,1)} %copy.49), calls=%async_computation.6 | async-start | bytes 3145728 | tf_op jit(solution)/shard_map/all_to_all | solution.py:65
  457.5 26.5 %all-to-all-start.5 = ((bf16[32,32,768]{2,0,1:T(8,128)(2,1)}), bf16[32,32,768]{2,0,1:T(8,128)(2,1)}, u32[]{:S(2)}, u32[]{:S(2)}) async-start(bf16[32,32,768]{2,0,1:T(8,128)(2,1)} %copy.47), calls=%async_computation.5 | async-start | bytes 3145728 | tf_op jit(solution)/shard_map/all_to_all | solution.py:64
  484.0 36.7 %all-to-all-start.4 = ((bf16[32,32,768]{2,0,1:T(8,128)(2,1)}), bf16[32,32,768]{2,0,1:T(8,128)(2,1)}, u32[]{:S(2)}, u32[]{:S(2)}) async-start(bf16[32,32,768]{2,0,1:T(8,128)(2,1)} %copy.45), calls=%async_computation.4 | async-start | bytes 3145728 | tf_op jit(solution)/shard_map/all_to_all | solution.py:66
  526.1 5.5 copy-start.5
  563.8 1.6 copy-start.8
  600.0 5.4 copy-start.4
  605.4 3.6 copy-start.1
Sparse Core Ops, SparseCore 0:
  85.1 124.1 all-reduce.2
  211.8 158.4 all-reduce.4
